TPU v7x, 32 devices: a whole 2x2x4 slice. The times are simulated.
32 devices in a mesh: dp: 2 (over x), context: 16 (over z, y, core).
Axes of the slice: x: 2, y: 2, z: 4, core: 2. Of those that a mesh axis runs over, the one named last changes fastest.
Arguments:
- grad_out: bfloat16 [2, 2048, 4096], P('dp', 'context'), may hold values from -6 to 6
- attn: bfloat16 [2, 2048, 4096], P('dp', 'context'), may hold values from -0.09375 to 0.09375
- w_out: bfloat16 [4096, 4096], P('context'), may hold values from -0.09375 to 0.09375
Outputs:
- grad_attn: bfloat16 [2, 2048, 4096], P('dp', None, 'context')
- grad_w: bfloat16 [4096, 4096], P('context')
All inputs are finite; a program needn't handle non-finite values.
Results may differ from a plain program's by a relative error of at most 0.013.
Values may be sent and summed in bfloat16 or wider, within the bound.
A program may use at most 128 MiB of HBM per device.

v0:
```python
import functools

import jax
import jax.numpy as jnp
from jax import lax
from jax.experimental import pallas as pl
from jax.experimental.pallas import tpu as pltpu
from jax.sharding import PartitionSpec as P

CHUNKS = 16
AHEAD = 3
AHEAD_Y = 8
CORES = 2
SIDE = 2
ACT0 = 1
RELAY = 3
FIRST = 2
BEGIN = 7
HOP = 1
PLANE = 1
MESH = pl.DeviceIdType.MESH


def grid_of(chips):
    fast = 1
    while (2 * fast) * (2 * fast) <= chips:
        fast *= 2
    return chips // fast, fast


def side_rows(tokens):
    return tokens * SIDE // 16


def kernel(dp, n, chunks, g_in, a_in, w_in, o_attn, o_w, gath, acts, acts_t, w, acc, part,
           relay, z_send, z_recv, p_recv, ys_send, y_recv, f_recv, s_recv, a_send, a_recv, r_send, r_recv, x_send, x_recv,
           own_sem, w_sem, own_a_sem):
    A, B = grid_of(n // CORES)
    tokens, width = g_in.shape
    heads = w_in.shape[0]
    F = width // chunks
    side = side_rows(tokens)
    line = A * tokens
    half = B * line
    me = lax.axis_index("context")
    rep = lax.axis_index("dp")
    c = lax.rem(me, CORES)
    b = lax.rem(me // CORES, B)
    a = me // (CORES * B)

    def ctx(a_, b_, c_):
        return (a_ * B + b_) * CORES + c_

    def others(i, size):
        return [lax.rem(i + d, size) for d in range(1, size)]

    def slot(i, t):
        s, bit = 0, 1
        while bit < A:
            s = s + bit * lax.rem(i // bit + t // bit, 2)
            bit *= 2
        return s

    pair = a + 1 - 2 * lax.rem(a, 2)

    def cols(k):
        return pl.ds(pl.multiple_of(k * F, F), F)

    def place(c_, u, s):
        return ((c_ * B + u) * A + s) * tokens

    def rows(k, lo, size):
        return gath.at[k, pl.ds(pl.multiple_of(lo, 8), size)]

    def own(k):
        return g_in.at[:, cols(k)]

    def remote(src, dst, send, recv, target):
        return pltpu.make_async_remote_copy(
            src_ref=src, dst_ref=dst, send_sem=send, recv_sem=recv, device_id=target, device_id_type=MESH)

    def inside(t):
        return jnp.logical_and(t >= 0, t < A)

    def own_copy(k):
        return pltpu.make_async_copy(own(k), rows(k, place(c, b, 0), tokens), own_sem.at[k])

    w_copy = pltpu.make_async_copy(w_in, w, w_sem)

    def head_cols(j):
        return pl.ds(pl.multiple_of(j * heads, heads), heads)

    own_act = pltpu.make_async_copy(a_in.at[:, head_cols(me)], acts.at[(c * B + b) * A], own_a_sem)

    barrier = pltpu.get_barrier_semaphore()
    for j in others(me, n):
        pl.semaphore_signal(barrier, inc=1, device_id={"context": j}, device_id_type=MESH)
    for r in others(rep, dp):
        pl.semaphore_signal(barrier, inc=1, device_id={"dp": r}, device_id_type=MESH)
    own_act.start()
    w_copy.start()

    @pl.loop(0, chunks)
    def _(k):
        own_copy(k).start()

    pl.semaphore_wait(barrier, n - 1 + dp - 1)

    edge = jnp.logical_or(a == 0, a == A - 1)

    def by_row(f, outer, inner):
        pl.when(edge)(lambda: f(outer))
        pl.when(jnp.logical_not(edge))(lambda: f(inner))

    def z_move(src, k, t, target):
        s = slot(target, t)
        return remote(src, rows(k, place(c, b, s), tokens), z_send.at[k], z_recv.at[k, s],
                      {"context": ctx(target, b, c)})

    def z_own(k):
        for sign in (1, -1):
            @pl.when(inside(a + sign))
            def _():
                z_move(own(k), k, a, a + sign).start()

    def y_own(k):
        for u in others(b, B):
            remote(own(k), rows(k, place(c, b, 0), tokens), ys_send.at[k], y_recv.at[k, b],
                   {"context": ctx(a, u, c)}).start()

    def side_moves(k):
        for u in others(b, B):
            got = rows(k, place(c, u, 0), tokens)
            remote(got, got, ys_send.at[k], y_recv.at[k, u], {"context": me}).wait_recv()
            by_row(lambda size, u=u: remote(
                rows(k, place(c, u, 0), size), rows(k, place(c, u, 1), size), z_send.at[k], p_recv.at[k, u],
                {"context": ctx(pair, b, c)}).start(), tokens, side)

    def column_moves(k, d):
        for sign in (1, -1):
            t = a + sign * d

            @pl.when(inside(t))
            def _():
                s = slot(a, t)
                got = rows(k, place(c, b, s), tokens)
                remote(got, got, z_send.at[k], z_recv.at[k, s], {"context": me}).wait_recv()

                @pl.when(inside(a - sign))
                def _():
                    z_move(got, k, t, a - sign).start()

    def to_sibling(k, u):
        whole = rows(k, place(c, u, 0), line)
        remote(whole, whole, ys_send.at[k], s_recv.at[k], {"context": ctx(a, b, 1 - c)}).start()

    def across(k, s):
        def send(skip):
            if skip < tokens:
                ref = rows(k, place(c, b, s) + skip, tokens - skip)
                for u in others(b, B):
                    remote(ref, ref, ys_send.at[k], f_recv.at[k, b], {"context": ctx(a, u, c)}).start()
        if s == 1:
            by_row(send, side, tokens)
        else:
            send(0)

    def line_moves(k):
        own_copy(k).wait()
        to_sibling(k, b)

    def plane_moves(k):
        for u in others(b, B):
            def wait(size, u=u):
                late = rows(k, place(c, u, 1), size)
                remote(late, late, z_send.at[k], p_recv.at[k, u], {"context": me}).wait_recv()
                rest = rows(k, place(c, u, 1) + size, line - tokens - size)
                remote(rest, rest, ys_send.at[k], f_recv.at[k, u], {"context": me}).wait_recv()
            by_row(wait, side, tokens)
            to_sibling(k, u)

    def act_move(target):
        where = (c * B + b) * A + slot(target // (CORES * B), a)
        return remote(a_in.at[:, head_cols(target)], acts.at[where], a_send, a_recv, {"context": target})

    def x_moves(k):
        for r in others(rep, dp):
            remote(part.at[rep, k], part.at[rep, k], x_send.at[k], x_recv.at[k], {"dp": r}).start()

    for k in range(AHEAD):
        z_own(k)
    def edges():
        return [(e, c_) for e in range(2) for c_ in range(CORES)]

    def relay_out():
        for u in others(b, B):
            for e, c_ in edges():
                remote(a_in.at[:, head_cols(ctx(e * (A - 1), u, c_))], relay.at[b, e, c_], a_send, r_recv.at[b],
                       {"context": ctx(a, u, c)}).start()

    def relay_on():
        for u in others(b, B):
            remote(relay.at[u], relay.at[u], a_send, r_recv.at[u], {"context": me}).wait_recv()
            for e, c_ in edges():
                remote(relay.at[u, e, c_], acts.at[(c * B + u) * A + slot(e * (A - 1), a)], r_send, a_recv,
                       {"context": ctx(e * (A - 1), b, c_)}).start()

    def inner(f, also=True):
        if A > 2:
            pl.when(jnp.logical_and(jnp.logical_not(edge), also))(f)

    act_move(ctx(a, b, 1 - c)).start()
    for k in range(AHEAD_Y):
        if k == FIRST:
            inner(relay_out)
        y_own(k)

    depth = HOP * (A - 2)
    lag = depth + PLANE + 1
    chips = n // CORES
    batch = -(-(chips - 1) // (lag - ACT0))

    def act_moves(i):
        for q in range(batch):
            d = (i - ACT0) * batch + q + 1
            to = lax.rem(me // CORES + d, chips)
            direct = jnp.logical_and(i >= ACT0, d < chips)
            if A > 2:
                t = to // B
                last = jnp.logical_or(t == 0, t == A - 1)
                direct = jnp.logical_and(direct, jnp.logical_or(
                    edge, jnp.logical_or(jnp.logical_not(last), lax.rem(to, B) == b)))

            @pl.when(direct)
            def _():
                for c_ in range(CORES):
                    act_move(to * CORES + c_).start()
        inner(relay_on, i == RELAY)

    def ready(k):
        theirs = rows(k, place(1 - c, 0, 0), half)
        remote(theirs, theirs, ys_send.at[k], s_recv.at[k], {"context": me}).wait_recv()

    def weights(k):
        @pl.when(k == 0)
        def _():
            own_act.wait()
            most = acts.at[pl.ds(0, n - 1)]
            remote(most, most, a_send, a_recv, {"context": me}).wait_recv()
            for j in range(n):
                acts_t[:, j * tokens:(j + 1) * tokens] = acts[j].T

        part[rep, k] = jnp.dot(acts_t[...], gath[k], preferred_element_type=jnp.float32).astype(part.dtype)
        x_moves(k)

    def inputs(k):
        @pl.when(k == 0)
        def _():
            w_copy.wait()
            acc[...] = jnp.zeros_like(acc)

        @pl.loop(0, CORES * B)
        def _(i):
            r = pl.ds(pl.multiple_of(i * line, line), line)
            total = acc[r] + lax.dot_general(
                gath[k, r], w[:, cols(k)], (((1,), (1,)), ((), ())), preferred_element_type=jnp.float32)

            @pl.when(k < chunks - 1)
            def _():
                acc[r] = total

            @pl.when(k == chunks - 1)
            def _():
                c_, u = i // B, lax.rem(i, B)
                for s in range(A):
                    to = ctx(slot(a, s), u, c_) * tokens
                    o_attn[pl.ds(pl.multiple_of(to, tokens), tokens)] = total[
                        s * tokens:(s + 1) * tokens].astype(o_attn.dtype)

    def finish(k):
        last = part.at[pl.ds(0, dp - 1), k]
        remote(last, last, x_send.at[k], x_recv.at[k], {"dp": rep}).wait_recv()
        total = part[0, k].astype(jnp.float32)
        for r in range(1, dp):
            total += part[r, k].astype(jnp.float32)
        o_w[:, cols(k)] = total.astype(o_w.dtype)

    def sent(ref, sem):
        remote(ref, ref, sem, s_recv.at[0], {"context": me}).wait_send()

    def drain(k):
        by_row(lambda size: sent(rows(k, 0, half + (B - 1) * (line - size)), ys_send.at[k]), side, tokens)
        sent(part.at[pl.ds(0, dp - 1), k], x_send.at[k])

        by_row(lambda size: sent(rows(k, 0, size), z_send.at[k]), B * tokens, (A + 1) * tokens + (B - 1) * side)

    def stage(k, f):
        pl.when(jnp.logical_and(k >= 0, k < chunks))(functools.partial(f, k))

    def summed(i):
        return jnp.clip(jnp.minimum(i - lag + 1, 2 * (i - BEGIN + 1)), 0, chunks)

    @pl.loop(0, chunks + lag + 1)
    def _(i):
        for d in range(A - 1, 0, -1):
            stage(i - HOP * (d - 1), lambda k, d=d: column_moves(k, d))
            stage(i - HOP * (d - 1), lambda k, d=d: across(k, d))
        stage(i, side_moves)
        stage(i + AHEAD, z_own)
        stage(i + AHEAD_Y, y_own)
        act_moves(i)
        stage(i - depth, line_moves)
        stage(i - lag, ready)

        @pl.loop(summed(i - 1), summed(i))
        def _(k):
            weights(k)

        stage(i - lag, inputs)
        stage(i - depth - PLANE, plane_moves)

        @pl.loop(summed(i - 2), summed(i - 1))
        def _(k):
            finish(k)
            drain(k)

    sent(acts.at[pl.ds(0, n - 1)], a_send)
    inner(lambda: sent(relay.at[pl.ds(0, B - 1)], r_send))


def store(h, gw, o_h, o_gw, sem):
    moves = [pltpu.make_async_copy(h, o_h, sem.at[0]), pltpu.make_async_copy(gw, o_gw, sem.at[1])]
    for m in moves:
        m.start()
    for m in moves:
        m.wait()


def local(dp, n, grad_out, attn, w_out):
    g, x = grad_out[0], attn[0]
    tokens, width = g.shape
    heads = w_out.shape[0]
    length = tokens * n
    chunks = CHUNKS
    F = width // chunks
    A, B = grid_of(n // CORES)
    scratch = 2 * (length * width + 2 * length * heads + heads * width * (1 + dp)) + 4 * length * heads
    limit = min(52 * 2**20, scratch + 10 * 2**20)
    any_ = pl.BlockSpec(memory_space=pl.ANY)
    vmem = pl.BlockSpec(memory_space=pltpu.VMEM)
    bf = jnp.bfloat16
    dma = pltpu.SemaphoreType.DMA
    h, gw = pl.pallas_call(
        functools.partial(kernel, dp, n, chunks),
        out_shape=(jax.ShapeDtypeStruct((length, heads), bf), jax.ShapeDtypeStruct((heads, width), bf)),
        in_specs=[any_] * 3,
        out_specs=(vmem, vmem),
        scratch_shapes=[
            pltpu.VMEM((chunks, length, F), bf),
            pltpu.VMEM((n, tokens, heads), bf),
            pltpu.VMEM((heads, length), bf),
            pltpu.VMEM((heads, width), bf),
            pltpu.VMEM((length, heads), jnp.float32),
            pltpu.VMEM((dp, chunks, heads, F), bf),
            pltpu.VMEM((B, 2, CORES, tokens, heads), bf),
            dma((chunks,)), dma((chunks, A)), dma((chunks, B)), dma((chunks,)), dma((chunks, B)), dma((chunks, B)),
            dma((chunks,)), dma, dma, dma, dma((B,)), dma((chunks,)), dma((chunks,)),
            dma((chunks,)), dma, dma,
        ],
        compiler_params=pltpu.CompilerParams(
            collective_id=0, has_side_effects=True, vmem_limit_bytes=limit),
    )(*[pltpu.with_memory_space_constraint(v, pltpu.HBM) for v in (g, x, w_out)])
    h, gw = pl.pallas_call(
        store,
        out_shape=(jax.ShapeDtypeStruct((length, heads), bf), jax.ShapeDtypeStruct((heads, width), bf)),
        in_specs=[any_] * 2,
        out_specs=(any_, any_),
        scratch_shapes=[dma((2,))],
        compiler_params=pltpu.CompilerParams(vmem_limit_bytes=8 * 2**20),
    )(h, gw)
    return h[None], gw


def solution(mesh):
    dp, n = mesh.shape["dp"], mesh.shape["context"]
    in_specs = (P("dp", "context", None), P("dp", "context", None), P("context", None))
    out_specs = (P("dp", None, "context"), P("context", None))
    return jax.shard_map(functools.partial(local, dp, n), mesh=mesh, in_specs=in_specs, out_specs=out_specs,
                         check_vma=False)
```

profile of v0, /device:TPU:0, one launch (start us, length us, event | category | flops | bytes accessed | tf_op | source)
XLA Modules:
  0.0 113.9 jit_solution(7110573577359475021)
XLA Ops:
  0.6 111.6 %shard_map.50 = (bf16[2048,256]{1,0:T(8,128)(2,1)S(1)}, bf16[256,4096]{1,0:T(8,128)(2,1)S(1)}) custom-call(bf16[128,4096]{1,0:T(8,128)(2,1)} %bitcast.3, bf16[128,4096]{1,0:T(8,128)(2,1)} %bitcast.4, bf16[256,4096]{1,0:T(8,128)(2,1)} %w_in.1), custom_call_target="tpu_custom_call" | custom-call | tf_op jit(solution)/shard_map/pallas_call | solution.py:353
  112.2 1.7 %shard_map.51 = (bf16[2048,256]{1,0:T(8,128)(2,1)}, bf16[256,4096]{1,0:T(8,128)(2,1)}) custom-call(bf16[2048,256]{1,0:T(8,128)(2,1)S(1)} %get-tuple-element.6.h, bf16[256,4096]{1,0:T(8,128)(2,1)S(1)} %get-tuple-element.7.gw), custom_call_target="tpu_custom_call" | custom-call | tf_op jit(solution)/shard_map/pallas_call | solution.py:373
where the time goes:
time: 114 us
  Pallas kernels  113 us (99%)
    pallas_call x1, Pallas kernels, local(): pl.pallas_call(functools.partial(kernel, dp, n, chunks), out_shape=(jax.S...  112 us

commit v1 on v0

--- a/solution.py
+++ b/solution.py
@@ -14,7 +14,7 @@
 SIDE = 2
 ACT0 = 1
 RELAY = 3
-FIRST = 2
+FIRST = 4
 BEGIN = 7
 HOP = 1
 PLANE = 1
@@ -300,15 +300,15 @@
     def summed(i):
         return jnp.clip(jnp.minimum(i - lag + 1, 2 * (i - BEGIN + 1)), 0, chunks)
 
-    @pl.loop(0, chunks + lag + 1)
+    @pl.loop(0, chunks + lag + 2)
     def _(i):
         for d in range(A - 1, 0, -1):
             stage(i - HOP * (d - 1), lambda k, d=d: column_moves(k, d))
             stage(i - HOP * (d - 1), lambda k, d=d: across(k, d))
         stage(i, side_moves)
+        act_moves(i)
         stage(i + AHEAD, z_own)
         stage(i + AHEAD_Y, y_own)
-        act_moves(i)
         stage(i - depth, line_moves)
         stage(i - lag, ready)
 
@@ -319,7 +319,7 @@
         stage(i - lag, inputs)
         stage(i - depth - PLANE, plane_moves)
 
-        @pl.loop(summed(i - 2), summed(i - 1))
+        @pl.loop(summed(i - 3), summed(i - 2))
         def _(k):
             finish(k)
             drain(k)
@@ -329,7 +329,12 @@
 
 
 def store(h, gw, o_h, o_gw, sem):
-    moves = [pltpu.make_async_copy(h, o_h, sem.at[0]), pltpu.make_async_copy(gw, o_gw, sem.at[1])]
+    moves, half = [], sem.shape[0] // 2
+    for src, dst in ((gw, o_gw), (h, o_h)):
+        size = src.shape[0] // half
+        for i in range(half):
+            r = pl.ds(i * size, size)
+            moves.append(pltpu.make_async_copy(src.at[r], dst.at[r], sem.at[len(moves)]))
     for m in moves:
         m.start()
     for m in moves:
@@ -375,7 +380,7 @@
         out_shape=(jax.ShapeDtypeStruct((length, heads), bf), jax.ShapeDtypeStruct((heads, width), bf)),
         in_specs=[any_] * 2,
         out_specs=(any_, any_),
-        scratch_shapes=[dma((2,))],
+        scratch_shapes=[dma((8,))],
         compiler_params=pltpu.CompilerParams(vmem_limit_bytes=8 * 2**20),
     )(h, gw)
     return h[None], gw

time: 114 us -> 114 us (level)
  no operation moved by 1% of the time
where the time goes in v1:
time: 114 us
  Pallas kernels  113 us (99%)
    pallas_call x1, Pallas kernels, local(): pl.pallas_call(functools.partial(kernel, dp, n, chunks), out_shape=(jax.S...  111 us

profile of v1, /device:TPU:0, one launch (start us, length us, event | category | flops | bytes accessed | tf_op | source)
XLA Modules:
  0.0 113.8 jit_solution(5898376315167512502)
XLA Ops:
  0.6 111.5 %shard_map.50 = (bf16[2048,256]{1,0:T(8,128)(2,1)S(1)}, bf16[256,4096]{1,0:T(8,128)(2,1)S(1)}) custom-call(bf16[128,4096]{1,0:T(8,128)(2,1)} %bitcast.3, bf16[128,4096]{1,0:T(8,128)(2,1)} %bitcast.4, bf16[256,4096]{1,0:T(8,128)(2,1)} %w_in.1), custom_call_target="tpu_custom_call" | custom-call | tf_op jit(solution)/shard_map/pallas_call | solution.py:358
  112.1 1.7 %shard_map.51 = (bf16[2048,256]{1,0:T(8,128)(2,1)}, bf16[256,4096]{1,0:T(8,128)(2,1)}) custom-call(bf16[2048,256]{1,0:T(8,128)(2,1)S(1)} %get-tuple-element.6.h, bf16[256,4096]{1,0:T(8,128)(2,1)S(1)} %get-tuple-element.7.gw), custom_call_target="tpu_custom_call" | custom-call | tf_op jit(solution)/shard_map/pallas_call | solution.py:378

commit v2 on v0

--- a/solution.py
+++ b/solution.py
@@ -13,8 +13,8 @@
 CORES = 2
 SIDE = 2
 ACT0 = 1
-RELAY = 3
-FIRST = 2
+RELAY = 2
+FIRST = 4
 BEGIN = 7
 HOP = 1
 PLANE = 1

time: 114 us -> 114 us (level)
  no operation moved by 1% of the time
where the time goes in v2:
time: 114 us
  Pallas kernels  114 us (100%)
    pallas_call x1, Pallas kernels, local(): pl.pallas_call(functools.partial(kernel, dp, n, chunks), out_shape=(jax.S...  112 us

profile of v2, /device:TPU:0, one launch (start us, length us, event | category | flops | bytes accessed | tf_op | source)
XLA Modules:
  0.0 114.3 jit_solution(14851389194965423650)
XLA Ops:
  0.6 111.9 %shard_map.50 = (bf16[2048,256]{1,0:T(8,128)(2,1)S(1)}, bf16[256,4096]{1,0:T(8,128)(2,1)S(1)}) custom-call(bf16[128,4096]{1,0:T(8,128)(2,1)} %bitcast.3, bf16[128,4096]{1,0:T(8,128)(2,1)} %bitcast.4, bf16[256,4096]{1,0:T(8,128)(2,1)} %w_in.1), custom_call_target="tpu_custom_call" | custom-call | tf_op jit(solution)/shard_map/pallas_call | solution.py:353
  112.6 1.7 %shard_map.51 = (bf16[2048,256]{1,0:T(8,128)(2,1)}, bf16[256,4096]{1,0:T(8,128)(2,1)}) custom-call(bf16[2048,256]{1,0:T(8,128)(2,1)S(1)} %get-tuple-element.6.h, bf16[256,4096]{1,0:T(8,128)(2,1)S(1)} %get-tuple-element.7.gw), custom_call_target="tpu_custom_call" | custom-call | tf_op jit(solution)/shard_map/pallas_call | solution.py:373
